TPU v7x, 256 devices: a whole 4x4x8 slice. The times are simulated.
256 devices in a mesh: lon: 32 (over y_hi, z, core), lat: 8 (over x, y_lo).
Axes of the slice: x: 4, y: 4 (y_hi: 2, y_lo: 2; y = y_hi * 2 + y_lo), z: 8, core: 2. Of those that a mesh axis runs over, the one named last changes fastest.
Arguments:
- inputs: bfloat16 [256, 1024, 192], P('lat', 'lon'), may hold values from -6 to 6
- cotangent: bfloat16 [256, 1024, 192], P('lat', 'lon'), may hold values from -6 to 6
- first_weight: bfloat16 [3, 3, 192, 192], replicated, may hold values from -0.15625 to 0.15625
- second_weight: bfloat16 [3, 3, 192, 192], replicated, may hold values from -0.15625 to 0.15625
Outputs:
- input_gradient: bfloat16 [256, 1024, 192], P('lat', 'lon')
- first_kernel_gradient: float32 [3, 3, 192, 192], replicated
- second_kernel_gradient: float32 [3, 3, 192, 192], replicated
All inputs are finite; a program needn't handle non-finite values.
Results may differ from a plain program's by a relative error of at most 0.0049.
Values may be sent and summed in bfloat16 or wider, within the bound.
A program may use at most 128 MiB of HBM per device.

v0:
```python
import math
import jax
import jax.numpy as jnp
from jax import lax
from jax.sharding import PartitionSpec as P

FIRST_SPREAD = 32
SECOND_SPREAD = 64


def with_halo(cells, sides, width):
    for axis, dim in sides:
        count = lax.axis_size(axis)
        ends = count - 1
        head = lax.slice_in_dim(cells, 0, width, axis=dim)
        tail = lax.slice_in_dim(cells, cells.shape[dim] - width, cells.shape[dim], axis=dim)
        cells = jnp.concatenate(
            [
                lax.ppermute(tail, axis, [(i, (i + 1) % count) for i in range(ends)]),
                cells,
                lax.ppermute(head, axis, [((i + 1) % count, i) for i in range(ends)]),
            ],
            axis=dim,
        )
    return cells


def from_behind(value, axis, steps):
    count = lax.axis_size(axis)
    pairs = [(source, (source + steps) % count) for source in range(count)]
    return lax.ppermute(value, axis, pairs)


def widened_field(field, dilation):
    rimmed = with_halo(field, (("lat", 0),), 1)
    border_width = field.shape[1]
    reach = -(-dilation // border_width)
    behind = []
    ahead_list = []
    for distance in range(reach, 0, -1):
        behind.append(from_behind(rimmed, "lon", distance))
    for distance in range(1, reach + 1):
        ahead_list.append(from_behind(rimmed, "lon", -distance))
    return (jnp.concatenate(behind + [rimmed] + ahead_list, axis=1), dilation)


def gather_taps(extended, offset, dilation, border_width):
    height = extended.shape[0] - 2
    pieces = []
    for row_off in range(3):
        for col_off in (-1, 0, 1):
            start = offset + col_off * dilation
            pieces.append(extended[row_off : row_off + height, start : start + border_width])
    return jnp.concatenate(pieces, axis=2).reshape(height * border_width, -1)


def flipped_kernel(weight):
    return jnp.transpose(weight[::-1, ::-1], (0, 1, 3, 2))


def contract_cells(stacked, other):
    return lax.dot_general(
        stacked, other, (((0,), (0,)), ((), ())), preferred_element_type=jnp.float32
    )


def shards(inputs, cotangent, first_weight, second_weight):
    height, border_width, channels = inputs.shape
    gradient_scale = 1.0 / math.sqrt(
        height * lax.axis_size("lat") * border_width * lax.axis_size("lon")
    )
    extended_input, input_shift = widened_field(inputs, FIRST_SPREAD)
    input_taps = gather_taps(extended_input, input_shift, FIRST_SPREAD, border_width)
    pre_activation = jnp.dot(
        input_taps, first_weight.reshape(-1, channels), preferred_element_type=jnp.float32
    )
    hidden_state = (
        jax.nn.silu(pre_activation).astype(jnp.bfloat16).reshape(height, border_width, channels)
    )
    extended_hidden, hidden_shift = widened_field(hidden_state, SECOND_SPREAD)
    hidden_taps = gather_taps(extended_hidden, hidden_shift, SECOND_SPREAD, border_width)
    extended_cotangent, cotangent_shift = widened_field(cotangent, SECOND_SPREAD)
    cotangent_taps = gather_taps(extended_cotangent, cotangent_shift, SECOND_SPREAD, border_width)
    hidden_gradient = jnp.dot(
        cotangent_taps,
        flipped_kernel(second_weight).reshape(-1, channels),
        preferred_element_type=jnp.float32,
    )
    part_two = contract_cells(hidden_taps, cotangent.reshape(-1, channels))
    sigma = jax.nn.sigmoid(pre_activation)
    pre_flat = (hidden_gradient * sigma * (1.0 + pre_activation * (1.0 - sigma))).astype(
        jnp.bfloat16
    )
    pre_activation_gradient = pre_flat.reshape(height, border_width, channels)
    extended_pre_gradient, pre_gradient_shift = widened_field(pre_activation_gradient, FIRST_SPREAD)
    pre_gradient_taps = gather_taps(
        extended_pre_gradient, pre_gradient_shift, FIRST_SPREAD, border_width
    )
    input_gradient = jnp.dot(
        pre_gradient_taps,
        flipped_kernel(first_weight).reshape(-1, channels),
        preferred_element_type=jnp.float32,
    )
    input_gradient = input_gradient.astype(jnp.bfloat16).reshape(height, border_width, channels)
    part_one = contract_cells(input_taps, pre_flat)
    summed_one, summed_two = lax.psum((part_one, part_two), ("lon", "lat"))
    first_kernel_gradient = (summed_one * gradient_scale).reshape(3, 3, channels, channels)
    second_kernel_gradient = (summed_two * gradient_scale).reshape(3, 3, channels, channels)
    return (input_gradient, first_kernel_gradient, second_kernel_gradient)


def solution(mesh):
    placed = (P("lat", "lon", None), P("lat", "lon", None), P(), P())
    return jax.shard_map(
        shards,
        mesh=mesh,
        in_specs=placed,
        out_specs=(P("lat", "lon", None), P(), P()),
        check_vma=False,
    )
```

profile of v0, /device:TPU:97, one launch (start us, length us, event | category | flops | bytes accessed | tf_op | source)
XLA Modules:
  0.0 406.2 jit_solution(7806731082396063454)
XLA Ops:
  8.0 3.2 collective-permute-start.4
  13.3 4.0 collective-permute-start
  20.4 2.8 pad_maximum_fusion.6
  28.2 2.7 collective-permute-start.6
  33.4 2.7 collective-permute-start.2
  37.3 2.8 collective-permute-done.6
  41.3 6.9 %concatenate.72 = bf16[32,32,1728]{2,1,0:T(8,128)(2,1)} concatenate(bf16[32,32,192]{2,1,0:T(8,128)(2,1)} %get-tuple-element.25, bf16[32,32,192]{2,1,0:T(8,128)(2,1)} %get-tuple-element.38, bf16[32,32,192]{2,1,0:T(8,128)(2,1)} %get-tuple-element.22, bf16[32,32,192]{2,1,0:T(8,128)(2,1)} %get-tuple-element.24, bf16[32,32,192]{2,1,0:T(8,128)(2,1)S(1)} %copy-done.3, ...), dimensions={2} | concatenate | bytes 7077888 | tf_op jit(solution)/shard_map/concatenate | solution.py:54
  49.3 4.7 %multiply_convert_fusion = (bf16[1024,192]{0,1:T(8,128)(2,1)}, f32[1024,192]{0,1:T(8,128)}) fusion(bf16[1024,1728]{1,0:T(8,128)(2,1)} %bitcast.42, bf16[1728,192]{1,0:T(8,128)(2,1)} %bitcast.60), kind=kOutput, calls=%fused_computation.7 | convolution fusion | flops 680460288 | bytes 5382144 | tf_op jit(solution)/shard_map/dot_general | solution.py:74
  55.2 6.6 %concatenate.68 = bf16[32,32,1728]{2,1,0:T(8,128)(2,1)} concatenate(bf16[32,32,192]{2,1,0:T(8,128)(2,1)} %get-tuple-element.31, bf16[32,32,192]{2,1,0:T(8,128)(2,1)S(1)} %copy-done.5, bf16[32,32,192]{2,1,0:T(8,128)(2,1)} %get-tuple-element.28, bf16[32,32,192]{2,1,0:T(8,128)(2,1)} %get-tuple-element.30, bf16[32,32,192]{2,1,0:T(8,128)(2,1)S(1)} %copy-done, ...), dimensions={2} | concatenate | bytes 7077888 | tf_op jit(solution)/shard_map/concatenate | solution.py:54
  61.8 4.0 fusion.1
  65.9 4.5 %collective-permute-start.8 = (bf16[1,32,192]{1,2,0:T(8,128)(2,1)S(1)}, bf16[1,32,192]{1,2,0:T(8,128)(2,1)S(1)}, u32[]{:S(2)}, u32[]{:S(2)}) collective-permute-start(bf16[1,32,192]{1,2,0:T(8,128)(2,1)S(1)} %get-tuple-element.48), channel_id=1, source_target_pairs={{0,1},{1,2},{2,3},{3,4},{4,5},{5,6},{6,7},{8,9},{9,10},{10,11},{11... | collective-permute-start | bytes 36872 | tf_op jit(solution)/shard_map/ppermute | solution.py:19
  72.1 5.2 %collective-permute-start.12 = (bf16[1,32,192]{1,2,0:T(8,128)(2,1)S(1)}, bf16[1,32,192]{1,2,0:T(8,128)(2,1)S(1)}, u32[]{:S(2)}, u32[]{:S(2)}) collective-permute-start(bf16[1,32,192]{1,2,0:T(8,128)(2,1)S(1)} %get-tuple-element.46), channel_id=1, source_target_pairs={{0,1},{1,2},{2,3},{3,4},{4,5},{5,6},{6,7},{8,9},{9,10},{10,11},{11... | collective-permute-start | bytes 36872 | tf_op jit(solution)/shard_map/ppermute | solution.py:19
  79.7 4.1 %collective-permute-start.10 = (bf16[34,32,192]{2,1,0:T(8,128)(2,1)}, bf16[34,32,192]{2,1,0:T(8,128)(2,1)S(1)}, u32[]{:S(2)}, u32[]{:S(2)}) collective-permute-start(bf16[34,32,192]{2,1,0:T(8,128)(2,1)} %pad_maximum_fusion), channel_id=1, source_target_pairs={{0,8},{8,16},{16,24},{24,32},{32,40},{40,48},{48,56},{56,64},{64,7... | collective-permute-start | bytes 1253384 | tf_op jit(solution)/shard_map/ppermute | solution.py:31
  83.9 4.0 fusion.12
  89.2 2.7 collective-permute-start.14
  93.0 2.0 copy.29
  95.0 2.0 copy.34
  99.3 2.1 copy.28
  101.4 3.6 collective-permute-done.15
  107.4 6.9 %concatenate.88 = bf16[32,32,1728]{2,1,0:T(8,128)(2,1)} concatenate(bf16[32,32,192]{2,1,0:T(8,128)(2,1)} %get-tuple-element.13, bf16[32,32,192]{2,1,0:T(8,128)(2,1)} %get-tuple-element.33, bf16[32,32,192]{2,1,0:T(8,128)(2,1)} %get-tuple-element.10, bf16[32,32,192]{2,1,0:T(8,128)(2,1)} %get-tuple-element.12, bf16[32,32,192]{2,1,0:T(8,128)(2,1)S(1)} %bitcast.46, ...), dimensions={2} | concatenate | bytes 7077888 | tf_op jit(solution)/shard_map/concatenate | solution.py:54
  115.1 4.0 convolution_bitcast_fusion
  130.2 2.9 convolution_convert_fusion
  134.1 259.9 %all-reduce.3.cloned.1.call-done = (f32[1728,192]{0,1:T(8,128)}, f32[1728,192]{0,1:T(8,128)}) async-done(((f32[1728,192]{0,1:T(8,128)}, f32[1728,192]{0,1:T(8,128)}), (f32[1728,192]{0,1:T(8,128)}, f32[1728,192]{0,1:T(8,128)})) %all-reduce.3.cloned.1.call-update) | async-done | bytes 2654224 | tf_op jit(solution)/shard_map/psum | solution.py:106
  394.0 1.9 broadcast_multiply_fusion
  (100 shorter events, 45.6 us)
Async XLA Ops:
  7.2 386.8 %all-reduce.3.cloned.1.call-start = ((), (), s32[]{:S(2)}) async-start(), calls=%async_computation | async-start | bytes 5505024 | tf_op jit(solution)/shard_map/psum | solution.py:106
  7.2 18.2 %copy-start.11 = (bf16[3,3,192,192]{3,2,1,0:T(8,128)(2,1)S(1)}, bf16[3,3,192,192]{3,2,1,0:T(8,128)(2,1)}, u32[]{:S(2)}) copy-start(bf16[3,3,192,192]{3,2,1,0:T(8,128)(2,1)} %param.6) | copy-start | bytes 1990660
  8.0 11.8 %collective-permute-start.4 = (bf16[1,32,192]{2,1,0:T(8,128)(2,1)S(1)}, bf16[1,32,192]{2,1,0:T(8,128)(2,1)S(1)}, u32[]{:S(2)}, u32[]{:S(2)}) collective-permute-start(bf16[1,32,192]{2,1,0:T(8,128)(2,1)S(1)} %get-tuple-element.40), channel_id=1, source_target_pairs={{0,1},{1,2},{2,3},{3,4},{4,5},{5,6},{6,7},{8,9},{9,10},{10,11},{11... | collective-permute-start | bytes 36872 | tf_op jit(solution)/shard_map/ppermute | solution.py:19
  11.2 9.2 %collective-permute-start.5 = (bf16[1,32,192]{2,1,0:T(8,128)(2,1)S(1)}, bf16[1,32,192]{2,1,0:T(8,128)(2,1)S(1)}, u32[]{:S(2)}, u32[]{:S(2)}) collective-permute-start(bf16[1,32,192]{2,1,0:T(8,128)(2,1)S(1)} %get-tuple-element.39), channel_id=1, source_target_pairs={{1,0},{2,1},{3,2},{4,3},{5,4},{6,5},{7,6},{9,8},{10,9},{11,10},{12... | collective-permute-start | bytes 36872 | tf_op jit(solution)/shard_map/ppermute | solution.py:21
  13.3 17.7 %collective-permute-start = (bf16[1,32,192]{2,1,0:T(8,128)(2,1)S(1)}, bf16[1,32,192]{2,1,0:T(8,128)(2,1)S(1)}, u32[]{:S(2)}, u32[]{:S(2)}) collective-permute-start(bf16[1,32,192]{2,1,0:T(8,128)(2,1)S(1)} %get-tuple-element.45), channel_id=1, source_target_pairs={{0,1},{1,2},{2,3},{3,4},{4,5},{5,6},{6,7},{8,9},{9,10},{10,11},{11... | collective-permute-start | bytes 36872 | tf_op jit(solution)/shard_map/ppermute | solution.py:19
  17.3 14.3 %collective-permute-start.1 = (bf16[1,32,192]{2,1,0:T(8,128)(2,1)S(1)}, bf16[1,32,192]{2,1,0:T(8,128)(2,1)S(1)}, u32[]{:S(2)}, u32[]{:S(2)}) collective-permute-start(bf16[1,32,192]{2,1,0:T(8,128)(2,1)S(1)} %get-tuple-element.44), channel_id=1, source_target_pairs={{1,0},{2,1},{3,2},{4,3},{5,4},{6,5},{7,6},{9,8},{10,9},{11,10},{12... | collective-permute-start | bytes 36872 | tf_op jit(solution)/shard_map/ppermute | solution.py:21
  20.4 11.2 %copy-start = (bf16[32,32,192]{2,1,0:T(8,128)(2,1)S(1)}, bf16[32,32,192]{2,1,0:T(8,128)(2,1)}, u32[]{:S(2)}) copy-start(bf16[32,32,192]{2,1,0:T(8,128)(2,1)} %param.5) | copy-start | bytes 1179652
  23.9 12.2 %collective-permute-start.7 = (bf16[34,32,192]{2,1,0:T(8,128)(2,1)}, bf16[34,32,192]{2,1,0:T(8,128)(2,1)S(1)}, u32[]{:S(2)}, u32[]{:S(2)}) collective-permute-start(bf16[34,32,192]{2,1,0:T(8,128)(2,1)} %constant_dynamic-update-slice_fusion.3), channel_id=1, source_target_pairs={{0,248},{8,0},{16,8},{24,16},{32,24},{40,32},{48,40},{56,48},{64,5... | collective-permute-start | bytes 1253384 | tf_op jit(solution)/shard_map/ppermute | solution.py:31
  28.2 11.9 %collective-permute-start.6 = (bf16[34,32,192]{2,1,0:T(8,128)(2,1)}, bf16[34,32,192]{2,1,0:T(8,128)(2,1)S(1)}, u32[]{:S(2)}, u32[]{:S(2)}) collective-permute-start(bf16[34,32,192]{2,1,0:T(8,128)(2,1)} %constant_dynamic-update-slice_fusion.3), channel_id=1, source_target_pairs={{0,8},{8,16},{16,24},{24,32},{32,40},{40,48},{48,56},{56,64},{64,7... | collective-permute-start | bytes 1253384 | tf_op jit(solution)/shard_map/ppermute | solution.py:31
  32.8 8.5 %copy-start.3 = (bf16[32,32,192]{2,1,0:T(8,128)(2,1)S(1)}, bf16[32,32,192]{2,1,0:T(8,128)(2,1)}, u32[]{:S(2)}) copy-start(bf16[32,32,192]{2,1,0:T(8,128)(2,1)} %param.4) | copy-start | bytes 1179652
  33.4 14.8 %collective-permute-start.3 = (bf16[34,32,192]{2,1,0:T(8,128)(2,1)}, bf16[34,32,192]{2,1,0:T(8,128)(2,1)S(1)}, u32[]{:S(2)}, u32[]{:S(2)}) collective-permute-start(bf16[34,32,192]{2,1,0:T(8,128)(2,1)} %constant_dynamic-update-slice_fusion), channel_id=1, source_target_pairs={{0,240},{8,248},{16,0},{24,8},{32,16},{40,24},{48,32},{56,40},{64,... | collective-permute-start | bytes 1253384 | tf_op jit(solution)/shard_map/ppermute | solution.py:31
  33.4 20.6 %collective-permute-start.2 = (bf16[34,32,192]{2,1,0:T(8,128)(2,1)}, bf16[34,32,192]{2,1,0:T(8,128)(2,1)S(1)}, u32[]{:S(2)}, u32[]{:S(2)}) collective-permute-start(bf16[34,32,192]{2,1,0:T(8,128)(2,1)} %constant_dynamic-update-slice_fusion), channel_id=1, source_target_pairs={{0,16},{8,24},{16,32},{24,40},{32,48},{40,56},{48,64},{56,72},{64,... | collective-permute-start | bytes 1253384 | tf_op jit(solution)/shard_map/ppermute | solution.py:31
  61.8 10.0 %copy-start.13 = (bf16[1024,192]{0,1:T(8,128)(2,1)S(1)}, bf16[1024,192]{0,1:T(8,128)(2,1)}, u32[]{:S(2)}) copy-start(bf16[1024,192]{0,1:T(8,128)(2,1)} %get-tuple-element.50) | copy-start | bytes 1179652
  65.8 18.0 %copy-start.1 = (bf16[1024,192]{0,1:T(8,128)(2,1)}, bf16[1024,192]{0,1:T(8,128)(2,1)S(1)}, u32[]{:S(2)}) copy-start(bf16[1024,192]{0,1:T(8,128)(2,1)S(1)} %fusion.1) | copy-start | bytes 1179652
  65.9 12.6 %collective-permute-start.8 = (bf16[1,32,192]{1,2,0:T(8,128)(2,1)S(1)}, bf16[1,32,192]{1,2,0:T(8,128)(2,1)S(1)}, u32[]{:S(2)}, u32[]{:S(2)}) collective-permute-start(bf16[1,32,192]{1,2,0:T(8,128)(2,1)S(1)} %get-tuple-element.48), channel_id=1, source_target_pairs={{0,1},{1,2},{2,3},{3,4},{4,5},{5,6},{6,7},{8,9},{9,10},{10,11},{11... | collective-permute-start | bytes 36872 | tf_op jit(solution)/shard_map/ppermute | solution.py:19
  70.5 8.2 %collective-permute-start.9 = (bf16[1,32,192]{1,2,0:T(8,128)(2,1)S(1)}, bf16[1,32,192]{1,2,0:T(8,128)(2,1)S(1)}, u32[]{:S(2)}, u32[]{:S(2)}) collective-permute-start(bf16[1,32,192]{1,2,0:T(8,128)(2,1)S(1)} %get-tuple-element.49), channel_id=1, source_target_pairs={{1,0},{2,1},{3,2},{4,3},{5,4},{6,5},{7,6},{9,8},{10,9},{11,10},{12... | collective-permute-start | bytes 36872 | tf_op jit(solution)/shard_map/ppermute | solution.py:21
  72.1 16.0 %collective-permute-start.12 = (bf16[1,32,192]{1,2,0:T(8,128)(2,1)S(1)}, bf16[1,32,192]{1,2,0:T(8,128)(2,1)S(1)}, u32[]{:S(2)}, u32[]{:S(2)}) collective-permute-start(bf16[1,32,192]{1,2,0:T(8,128)(2,1)S(1)} %get-tuple-element.46), channel_id=1, source_target_pairs={{0,1},{1,2},{2,3},{3,4},{4,5},{5,6},{6,7},{8,9},{9,10},{10,11},{11... | collective-permute-start | bytes 36872 | tf_op jit(solution)/shard_map/ppermute | solution.py:19
  77.2 10.9 %collective-permute-start.13 = (bf16[1,32,192]{1,2,0:T(8,128)(2,1)S(1)}, bf16[1,32,192]{1,2,0:T(8,128)(2,1)S(1)}, u32[]{:S(2)}, u32[]{:S(2)}) collective-permute-start(bf16[1,32,192]{1,2,0:T(8,128)(2,1)S(1)} %get-tuple-element.47), channel_id=1, source_target_pairs={{1,0},{2,1},{3,2},{4,3},{5,4},{6,5},{7,6},{9,8},{10,9},{11,10},{12... | collective-permute-start | bytes 36872 | tf_op jit(solution)/shard_map/ppermute | solution.py:21
  79.7 18.4 %collective-permute-start.10 = (bf16[34,32,192]{2,1,0:T(8,128)(2,1)}, bf16[34,32,192]{2,1,0:T(8,128)(2,1)S(1)}, u32[]{:S(2)}, u32[]{:S(2)}) collective-permute-start(bf16[34,32,192]{2,1,0:T(8,128)(2,1)} %pad_maximum_fusion), channel_id=1, source_target_pairs={{0,8},{8,16},{16,24},{24,32},{32,40},{40,48},{48,56},{56,64},{64,7... | collective-permute-start | bytes 1253384 | tf_op jit(solution)/shard_map/ppermute | solution.py:31
  89.2 15.8 %collective-permute-start.15 = (bf16[34,32,192]{2,1,0:T(8,128)(2,1)}, bf16[34,32,192]{2,1,0:T(8,128)(2,1)S(1)}, u32[]{:S(2)}, u32[]{:S(2)}) collective-permute-start(bf16[34,32,192]{2,1,0:T(8,128)(2,1)} %pad_maximum_fusion.1), channel_id=1, source_target_pairs={{0,240},{8,248},{16,0},{24,8},{32,16},{40,24},{48,32},{56,40},{64,... | collective-permute-start | bytes 1253384 | tf_op jit(solution)/shard_map/ppermute | solution.py:31
  89.2 17.0 %collective-permute-start.14 = (bf16[34,32,192]{2,1,0:T(8,128)(2,1)}, bf16[34,32,192]{2,1,0:T(8,128)(2,1)S(1)}, u32[]{:S(2)}, u32[]{:S(2)}) collective-permute-start(bf16[34,32,192]{2,1,0:T(8,128)(2,1)} %pad_maximum_fusion.1), channel_id=1, source_target_pairs={{0,16},{8,24},{16,32},{24,40},{32,48},{40,56},{48,64},{56,72},{64,... | collective-permute-start | bytes 1253384 | tf_op jit(solution)/shard_map/ppermute | solution.py:31
  93.0 26.1 %collective-permute-start.11 = (bf16[34,32,192]{2,1,0:T(8,128)(2,1)}, bf16[34,32,192]{2,1,0:T(8,128)(2,1)S(1)}, u32[]{:S(2)}, u32[]{:S(2)}) collective-permute-start(bf16[34,32,192]{2,1,0:T(8,128)(2,1)} %pad_maximum_fusion), channel_id=1, source_target_pairs={{0,248},{8,0},{16,8},{24,16},{32,24},{40,32},{48,40},{56,48},{64,5... | collective-permute-start | bytes 1253384 | tf_op jit(solution)/shard_map/ppermute | solution.py:31
  99.3 8.1 %copy-start.4 = (bf16[32,32,192]{2,1,0:T(8,128)(2,1)S(1)}, bf16[32,32,192]{2,1,0:T(8,128)(2,1)}, u32[]{:S(2)}) copy-start(bf16[32,32,192]{2,1,0:T(8,128)(2,1)} %get-tuple-element.32) | copy-start | bytes 1179652
  121.9 8.3 %copy-start.12 = (bf16[3,3,192,192]{3,2,1,0:T(8,128)(2,1)S(1)}, bf16[3,3,192,192]{3,2,1,0:T(8,128)(2,1)}, u32[]{:S(2)}) copy-start(bf16[3,3,192,192]{3,2,1,0:T(8,128)(2,1)} %copy.36) | copy-start | bytes 1990660
  (7 other events, 30.4 us)
Sparse Core Ops, SparseCore 0:
  122.0 271.9 all-reduce.2
where the time goes:
time: 408 us; the launch traced here: 406 us
  waiting for transfers between devices  266 us (65%)
  local copies, waits for them, and re-layouts  59.8 us (15%)
  starting transfers between devices  35.8 us (9%)
  matrix products  19.7 us (5%)
  between operations  14.3 us (4%)
  other arithmetic  10.2 us (2%)
    psum x1, waiting for transfers between devices, shards(): summed_one, summed_two = lax.psum((part_one, part_two), ('lon', 'lat'))  260 us
    concatenate x12, local copies, waits for them, and re-layouts, gather_taps(): return jnp.concatenate(pieces, axis=2).reshape(height * border_width, -1)  29.8 us
    ppermute x4, starting transfers between devices, with_halo(): lax.ppermute(tail, axis, [(i, (i + 1) % count) for i in range(ends)])  16.9 us
    ppermute x8, starting transfers between devices, from_behind(): return lax.ppermute(value, axis, pairs)  13.8 us
    unnamed x38, local copies, waits for them, and re-layouts  9.53 us
    slice x8, local copies, waits for them, and re-layouts, gather_taps(): extended[row_off:row_off + height, start:start + border_width]  8.44 us
    concatenate x6, other arithmetic, with_halo(): jnp.concatenate([lax.ppermute(tail, axis, [(i, (i + 1) % count) for i in...  8.29 us
  transfers between devices with their start and end apart: 17, of which 3 were waited for; matrix products, arithmetic and copies ran while one was open for 17% of the time, Pallas kernels for 0%

commit v1 on v0

--- a/solution.py
+++ b/solution.py
@@ -103,7 +103,7 @@
     )
     input_gradient = input_gradient.astype(jnp.bfloat16).reshape(height, border_width, channels)
     part_one = contract_cells(input_taps, pre_flat)
-    summed_one, summed_two = lax.psum((part_one, part_two), ("lon", "lat"))
+    summed_one, summed_two = lax.psum(lax.psum((part_one, part_two), "lon"), "lat")
     first_kernel_gradient = (summed_one * gradient_scale).reshape(3, 3, channels, channels)
     second_kernel_gradient = (summed_two * gradient_scale).reshape(3, 3, channels, channels)
     return (input_gradient, first_kernel_gradient, second_kernel_gradient)

time: 408 us -> 533 us (1.31)
  waiting for transfers between devices: 266 us -> 403 us
  local copies, waits for them, and re-layouts: 59.8 us -> 53.7 us
    psum x1 -> x2, waiting for transfers between devices: 260 us -> 384 us  [the longest x1 268 us: shards(): lax.psum((part_one, part_two), 'lon')]
    ppermute x8, waiting for transfers between devices: 6.36 us -> 15.6 us  [from_behind(): return lax.ppermute(value, axis, pairs)]
  transfers between devices with their start and end apart: 17 -> 18, of which waited for: 3 -> 7; matrix products, arithmetic and copies ran while one was open for 17% -> 11% of each run, Pallas kernels for 0% -> 0%
where the time goes in v1:
time: 533 us; the launch traced here: 529 us
  waiting for transfers between devices  403 us (76%)
  local copies, waits for them, and re-layouts  53.7 us (10%)
  starting transfers between devices  33 us (6%)
  matrix products  17.5 us (3%)
  between operations  14.4 us (3%)
  other arithmetic  7.36 us (1%)
    psum x1, waiting for transfers between devices, shards(): lax.psum((part_one, part_two), 'lon')  268 us
    psum x1, waiting for transfers between devices, shards(): lax.psum(lax.psum((part_one, part_two), 'lon'), 'lat')  115 us
    concatenate x12, local copies, waits for them, and re-layouts, gather_taps(): return jnp.concatenate(pieces, axis=2).reshape(height * border_width, -1)  27.6 us
    ppermute x8, waiting for transfers between devices, from_behind(): return lax.ppermute(value, axis, pairs)  15.6 us
    ppermute x4, starting transfers between devices, with_halo(): lax.ppermute(tail, axis, [(i, (i + 1) % count) for i in range(ends)])  13.8 us
    ppermute x8, starting transfers between devices, from_behind(): return lax.ppermute(value, axis, pairs)  13.8 us
  transfers between devices with their start and end apart: 18, of which 7 were waited for; matrix products, arithmetic and copies ran while one was open for 11% of the time, Pallas kernels for 0%

profile of v1, /device:TPU:97, one launch (start us, length us, event | category | flops | bytes accessed | tf_op | source)
XLA Modules:
  0.0 529.0 jit_solution(12319656788214091988)
XLA Ops:
  8.0 3.2 collective-permute-start.4
  13.2 4.0 collective-permute-start
  19.2 2.8 pad_maximum_fusion.6
  26.6 2.7 collective-permute-start.6
  31.8 2.7 collective-permute-start.2
  35.7 2.8 collective-permute-done.6
  39.7 6.9 %concatenate.72 = bf16[32,32,1728]{2,1,0:T(8,128)(2,1)} concatenate(bf16[32,32,192]{2,1,0:T(8,128)(2,1)} %get-tuple-element.27, bf16[32,32,192]{2,1,0:T(8,128)(2,1)} %get-tuple-element.40, bf16[32,32,192]{2,1,0:T(8,128)(2,1)} %get-tuple-element.24, bf16[32,32,192]{2,1,0:T(8,128)(2,1)} %get-tuple-element.26, bf16[32,32,192]{2,1,0:T(8,128)(2,1)S(1)} %copy-done.1, ...), dimensions={2} | concatenate | bytes 7077888 | tf_op jit(solution)/shard_map/concatenate | solution.py:54
  46.6 4.5 multiply_convert_fusion
  51.3 4.7 collective-permute-start.12
  59.7 6.6 %concatenate.68 = bf16[32,32,1728]{2,1,0:T(8,128)(2,1)} concatenate(bf16[32,32,192]{2,1,0:T(8,128)(2,1)} %get-tuple-element.33, bf16[32,32,192]{2,1,0:T(8,128)(2,1)S(1)} %copy-done.2, bf16[32,32,192]{2,1,0:T(8,128)(2,1)} %get-tuple-element.30, bf16[32,32,192]{2,1,0:T(8,128)(2,1)} %get-tuple-element.32, bf16[32,32,192]{2,1,0:T(8,128)(2,1)S(1)} %copy-done, ...), dimensions={2} | concatenate | bytes 7077888 | tf_op jit(solution)/shard_map/concatenate | solution.py:54
  66.3 4.0 fusion.1
  71.0 2.7 collective-permute-start.14
  73.6 4.0 fusion.12
  77.8 7.5 %collective-permute-done.15 = bf16[34,32,192]{2,1,0:T(8,128)(2,1)S(1)} collective-permute-done((bf16[34,32,192]{2,1,0:T(8,128)(2,1)S(1)}, bf16[34,32,192]{2,1,0:T(8,128)(2,1)S(1)}, u32[]{:S(2)}, u32[]{:S(2)}) %collective-permute-start.15) | collective-permute-done | bytes 417824 | tf_op jit(solution)/shard_map/ppermute | solution.py:31
  87.7 6.8 %concatenate.88 = bf16[32,32,1728]{2,1,0:T(8,128)(2,1)} concatenate(bf16[32,32,192]{2,1,0:T(8,128)(2,1)} %get-tuple-element.15, bf16[32,32,192]{2,1,0:T(8,128)(2,1)S(1)} %get-tuple-element.35, bf16[32,32,192]{2,1,0:T(8,128)(2,1)} %get-tuple-element.12, bf16[32,32,192]{2,1,0:T(8,128)(2,1)} %get-tuple-element.14, bf16[32,32,192]{2,1,0:T(8,128)(2,1)S(1)} %bitcast.46, ...), dimensions={2} | concatenate | bytes 7077888 | tf_op jit(solution)/shard_map/concatenate | solution.py:54
  94.5 4.0 convolution_bitcast_fusion
  98.6 268.1 %all-reduce.5.cloned.1.call-done = (f32[1728,192]{0,1:T(8,128)}, f32[1728,192]{0,1:T(8,128)}) async-done(((f32[1728,192]{0,1:T(8,128)}, f32[1728,192]{0,1:T(8,128)}), (f32[1728,192]{0,1:T(8,128)}, f32[1728,192]{0,1:T(8,128)})) %all-reduce.5.cloned.1.call-update) | async-done | bytes 2654224 | tf_op jit(solution)/shard_map/psum | solution.py:106
  366.8 2.0 collective-permute-start.8
  370.6 3.9 collective-permute-done.9
  375.5 4.1 collective-permute-start.10
  383.5 2.9 collective-permute-done.10
  387.5 2.4 collective-permute-done.11
  391.0 2.0 copy.30
  401.4 115.4 %all-reduce.7.cloned.1.call-done = (f32[1728,192]{0,1:T(8,128)}, f32[1728,192]{0,1:T(8,128)}) async-done(((f32[1728,192]{0,1:T(8,128)}, f32[1728,192]{0,1:T(8,128)}), (f32[1728,192]{0,1:T(8,128)}, f32[1728,192]{0,1:T(8,128)})) %all-reduce.7.cloned.1.call-update) | async-done | bytes 2654224 | tf_op jit(solution)/shard_map/psum | solution.py:106
  (93 shorter events, 43.8 us)
Async XLA Ops:
  7.2 22.8 %copy-start = (bf16[32,32,192]{2,1,0:T(8,128)(2,1)S(1)}, bf16[32,32,192]{2,1,0:T(8,128)(2,1)}, u32[]{:S(2)}) copy-start(bf16[32,32,192]{2,1,0:T(8,128)(2,1)} %param.5) | copy-start | bytes 1179652
  7.2 359.6 %all-reduce.5.cloned.1.call-start = ((), (), s32[]{:S(2)}) async-start(), calls=%async_computation | async-start | bytes 5505024 | tf_op jit(solution)/shard_map/psum | solution.py:106
  8.0 10.5 %collective-permute-start.4 = (bf16[1,32,192]{2,1,0:T(8,128)(2,1)S(1)}, bf16[1,32,192]{2,1,0:T(8,128)(2,1)S(1)}, u32[]{:S(2)}, u32[]{:S(2)}) collective-permute-start(bf16[1,32,192]{2,1,0:T(8,128)(2,1)S(1)} %get-tuple-element.42), channel_id=1, source_target_pairs={{0,1},{1,2},{2,3},{3,4},{4,5},{5,6},{6,7},{8,9},{9,10},{10,11},{11... | collective-permute-start | bytes 36872 | tf_op jit(solution)/shard_map/ppermute | solution.py:19
  11.2 7.9 %collective-permute-start.5 = (bf16[1,32,192]{2,1,0:T(8,128)(2,1)S(1)}, bf16[1,32,192]{2,1,0:T(8,128)(2,1)S(1)}, u32[]{:S(2)}, u32[]{:S(2)}) collective-permute-start(bf16[1,32,192]{2,1,0:T(8,128)(2,1)S(1)} %get-tuple-element.41), channel_id=1, source_target_pairs={{1,0},{2,1},{3,2},{4,3},{5,4},{6,5},{7,6},{9,8},{10,9},{11,10},{12... | collective-permute-start | bytes 36872 | tf_op jit(solution)/shard_map/ppermute | solution.py:21
  13.2 16.1 %collective-permute-start = (bf16[1,32,192]{2,1,0:T(8,128)(2,1)S(1)}, bf16[1,32,192]{2,1,0:T(8,128)(2,1)S(1)}, u32[]{:S(2)}, u32[]{:S(2)}) collective-permute-start(bf16[1,32,192]{2,1,0:T(8,128)(2,1)S(1)} %get-tuple-element.47), channel_id=1, source_target_pairs={{0,1},{1,2},{2,3},{3,4},{4,5},{5,6},{6,7},{8,9},{9,10},{10,11},{11... | collective-permute-start | bytes 36872 | tf_op jit(solution)/shard_map/ppermute | solution.py:19
  17.2 12.8 %collective-permute-start.1 = (bf16[1,32,192]{2,1,0:T(8,128)(2,1)S(1)}, bf16[1,32,192]{2,1,0:T(8,128)(2,1)S(1)}, u32[]{:S(2)}, u32[]{:S(2)}) collective-permute-start(bf16[1,32,192]{2,1,0:T(8,128)(2,1)S(1)} %get-tuple-element.46), channel_id=1, source_target_pairs={{1,0},{2,1},{3,2},{4,3},{5,4},{6,5},{7,6},{9,8},{10,9},{11,10},{12... | collective-permute-start | bytes 36872 | tf_op jit(solution)/shard_map/ppermute | solution.py:21
  22.5 12.0 %collective-permute-start.7 = (bf16[34,32,192]{2,1,0:T(8,128)(2,1)}, bf16[34,32,192]{2,1,0:T(8,128)(2,1)S(1)}, u32[]{:S(2)}, u32[]{:S(2)}) collective-permute-start(bf16[34,32,192]{2,1,0:T(8,128)(2,1)} %constant_dynamic-update-slice_fusion.3), channel_id=1, source_target_pairs={{0,248},{8,0},{16,8},{24,16},{32,24},{40,32},{48,40},{56,48},{64,5... | collective-permute-start | bytes 1253384 | tf_op jit(solution)/shard_map/ppermute | solution.py:31
  26.6 11.9 %collective-permute-start.6 = (bf16[34,32,192]{2,1,0:T(8,128)(2,1)}, bf16[34,32,192]{2,1,0:T(8,128)(2,1)S(1)}, u32[]{:S(2)}, u32[]{:S(2)}) collective-permute-start(bf16[34,32,192]{2,1,0:T(8,128)(2,1)} %constant_dynamic-update-slice_fusion.3), channel_id=1, source_target_pairs={{0,8},{8,16},{16,24},{24,32},{32,40},{40,48},{48,56},{56,64},{64,7... | collective-permute-start | bytes 1253384 | tf_op jit(solution)/shard_map/ppermute | solution.py:31
  31.2 8.5 %copy-start.1 = (bf16[32,32,192]{2,1,0:T(8,128)(2,1)S(1)}, bf16[32,32,192]{2,1,0:T(8,128)(2,1)}, u32[]{:S(2)}) copy-start(bf16[32,32,192]{2,1,0:T(8,128)(2,1)} %param.4) | copy-start | bytes 1179652
  31.8 25.4 %collective-permute-start.3 = (bf16[34,32,192]{2,1,0:T(8,128)(2,1)}, bf16[34,32,192]{2,1,0:T(8,128)(2,1)S(1)}, u32[]{:S(2)}, u32[]{:S(2)}) collective-permute-start(bf16[34,32,192]{2,1,0:T(8,128)(2,1)} %constant_dynamic-update-slice_fusion), channel_id=1, source_target_pairs={{0,240},{8,248},{16,0},{24,8},{32,16},{40,24},{48,32},{56,40},{64,... | collective-permute-start | bytes 1253384 | tf_op jit(solution)/shard_map/ppermute | solution.py:31
  31.8 26.7 %collective-permute-start.2 = (bf16[34,32,192]{2,1,0:T(8,128)(2,1)}, bf16[34,32,192]{2,1,0:T(8,128)(2,1)S(1)}, u32[]{:S(2)}, u32[]{:S(2)}) collective-permute-start(bf16[34,32,192]{2,1,0:T(8,128)(2,1)} %constant_dynamic-update-slice_fusion), channel_id=1, source_target_pairs={{0,16},{8,24},{16,32},{24,40},{32,48},{40,56},{48,64},{56,72},{64,... | collective-permute-start | bytes 1253384 | tf_op jit(solution)/shard_map/ppermute | solution.py:31
  51.2 6.1 %copy-start.7 = (bf16[1024,192]{0,1:T(8,128)(2,1)}, bf16[1024,192]{0,1:T(8,128)(2,1)S(1)}, u32[]{:S(2)}) copy-start(bf16[1024,192]{0,1:T(8,128)(2,1)S(1)} %get-tuple-element.52) | copy-start | bytes 1179652
  51.2 8.5 %copy-start.2 = (bf16[32,32,192]{2,1,0:T(8,128)(2,1)S(1)}, bf16[32,32,192]{2,1,0:T(8,128)(2,1)}, u32[]{:S(2)}) copy-start(bf16[32,32,192]{2,1,0:T(8,128)(2,1)} %get-tuple-element.44) | copy-start | bytes 1179652
  51.3 19.3 %collective-permute-start.12 = (bf16[1,32,192]{1,2,0:T(8,128)(2,1)S(1)}, bf16[1,32,192]{1,2,0:T(8,128)(2,1)S(1)}, u32[]{:S(2)}, u32[]{:S(2)}) collective-permute-start(bf16[1,32,192]{1,2,0:T(8,128)(2,1)S(1)} %get-tuple-element.48), channel_id=1, source_target_pairs={{0,1},{1,2},{2,3},{3,4},{4,5},{5,6},{6,7},{8,9},{9,10},{10,11},{11... | collective-permute-start | bytes 36872 | tf_op jit(solution)/shard_map/ppermute | solution.py:19
  55.9 14.7 %collective-permute-start.13 = (bf16[1,32,192]{1,2,0:T(8,128)(2,1)S(1)}, bf16[1,32,192]{1,2,0:T(8,128)(2,1)S(1)}, u32[]{:S(2)}, u32[]{:S(2)}) collective-permute-start(bf16[1,32,192]{1,2,0:T(8,128)(2,1)S(1)} %get-tuple-element.49), channel_id=1, source_target_pairs={{1,0},{2,1},{3,2},{4,3},{5,4},{6,5},{7,6},{9,8},{10,9},{11,10},{12... | collective-permute-start | bytes 36872 | tf_op jit(solution)/shard_map/ppermute | solution.py:21
  70.9 14.4 %collective-permute-start.15 = (bf16[34,32,192]{2,1,0:T(8,128)(2,1)S(1)}, bf16[34,32,192]{2,1,0:T(8,128)(2,1)S(1)}, u32[]{:S(2)}, u32[]{:S(2)}) collective-permute-start(bf16[34,32,192]{2,1,0:T(8,128)(2,1)S(1)} %pad_maximum_fusion.1), channel_id=1, source_target_pairs={{0,240},{8,248},{16,0},{24,8},{32,16},{40,24},{48,32},{56,40},{64,... | collective-permute-start | bytes 1253384 | tf_op jit(solution)/shard_map/ppermute | solution.py:31
  71.0 15.6 %collective-permute-start.14 = (bf16[34,32,192]{2,1,0:T(8,128)(2,1)S(1)}, bf16[34,32,192]{2,1,0:T(8,128)(2,1)S(1)}, u32[]{:S(2)}, u32[]{:S(2)}) collective-permute-start(bf16[34,32,192]{2,1,0:T(8,128)(2,1)S(1)} %pad_maximum_fusion.1), channel_id=1, source_target_pairs={{0,16},{8,24},{16,32},{24,40},{32,48},{40,56},{48,64},{56,72},{64,... | collective-permute-start | bytes 1253384 | tf_op jit(solution)/shard_map/ppermute | solution.py:31
  98.5 418.3 %all-reduce.7.cloned.1.call-start = ((), (), s32[]{:S(2)}) async-start(), calls=%async_computation.1 | async-start | bytes 5505024 | tf_op jit(solution)/shard_map/psum | solution.py:106
  366.8 3.7 collective-permute-start.8
  368.8 5.7 %collective-permute-start.9 = (bf16[1,32,192]{1,2,0:T(8,128)(2,1)S(1)}, bf16[1,32,192]{1,2,0:T(8,128)(2,1)S(1)}, u32[]{:S(2)}, u32[]{:S(2)}) collective-permute-start(bf16[1,32,192]{1,2,0:T(8,128)(2,1)S(1)} %get-tuple-element.51), channel_id=1, source_target_pairs={{1,0},{2,1},{3,2},{4,3},{5,4},{6,5},{7,6},{9,8},{10,9},{11,10},{12... | collective-permute-start | bytes 36872 | tf_op jit(solution)/shard_map/ppermute | solution.py:21
  375.5 10.9 %collective-permute-start.10 = (bf16[34,32,192]{2,1,0:T(8,128)(2,1)}, bf16[34,32,192]{2,1,0:T(8,128)(2,1)S(1)}, u32[]{:S(2)}, u32[]{:S(2)}) collective-permute-start(bf16[34,32,192]{2,1,0:T(8,128)(2,1)} %pad_maximum_fusion), channel_id=1, source_target_pairs={{0,8},{8,16},{16,24},{24,32},{32,40},{40,48},{48,56},{56,64},{64,7... | collective-permute-start | bytes 1253384 | tf_op jit(solution)/shard_map/ppermute | solution.py:31
  379.6 10.4 %collective-permute-start.11 = (bf16[34,32,192]{2,1,0:T(8,128)(2,1)}, bf16[34,32,192]{2,1,0:T(8,128)(2,1)S(1)}, u32[]{:S(2)}, u32[]{:S(2)}) collective-permute-start(bf16[34,32,192]{2,1,0:T(8,128)(2,1)} %pad_maximum_fusion), channel_id=1, source_target_pairs={{0,248},{8,0},{16,8},{24,16},{32,24},{40,32},{48,40},{56,48},{64,5... | collective-permute-start | bytes 1253384 | tf_op jit(solution)/shard_map/ppermute | solution.py:31
  391.0 5.1 copy-start.3
  394.9 4.4 copy-start.4
  (3 other events, 10.9 us)
Sparse Core Ops, SparseCore 0:
  98.7 268.0 all-reduce.4
  369.4 147.3 all-reduce.6
